TPU v7x, 32 devices: a whole 2x2x4 slice. The times are simulated.
32 devices in a mesh: row: 8 (over y, x, core), col: 4 (over z).
Axes of the slice: x: 2, y: 2, z: 4, core: 2. Of those that a mesh axis runs over, the one named last changes fastest.
Arguments:
- matrix: float32 [8, 3, 256, 4, 6, 256], P('row', None, None, 'col'), as said below
- checksum: float32 [8, 3, 256, 6, 256], P('row'), as said below
- failed: int32 [4], P('col'), may hold values from 0 to 3, as said below
Outputs:
- factored: float32 [8, 3, 256, 4, 6, 256], P('row', None, None, 'col')
- updated_checksum_result: float32 [8, 3, 256, 6, 256], P('row')
Inputs may be any that keep to these rules, and one draw needn't show every extreme that they name: `failed`: a permutation of the grid column indices; entry 0 names the grid column whose tiles in matrix carry no information. With the lost grid column rebuilt from checksum, matrix is symmetric positive definite. `checksum`: for each grid row, the sum over all grid columns of the intact matrix's tiles, the lost column included.
All inputs are finite; a program needn't handle non-finite values.
Results may differ from a plain program's by a relative error of at most 0.0003.
Values sent between devices are 32-bit elements; how exact they have to be, the bound alone decides.
A program may use at most 128 MiB of HBM per device.

v0:
```python
import jax
import jax.numpy as jnp
from jax import lax
from jax.sharding import PartitionSpec as P

PANELS = 3
EXACT = lax.Precision.HIGHEST
FAST = lax.Precision.HIGH


def dot_t(a, b, precision=EXACT):
    return lax.dot_general(a, b, (((1,), (1,)), ((), ())), precision=precision)


def dot(a, b, precision=EXACT):
    return lax.dot_general(a, b, (((1,), (0,)), ((), ())), precision=precision)


def shards(matrix, checksum, failed):
    rows_count = lax.axis_size("row")
    cols_count = lax.axis_size("col")
    row_index = lax.axis_index("row")
    column_position = lax.axis_index("col")
    tile_rows, width, tile_cols = (matrix.shape[1], matrix.shape[2], matrix.shape[4])
    own = matrix.reshape(tile_rows, width, tile_cols, width).transpose(0, 2, 1, 3)
    totals = checksum.reshape(tile_rows, width, tile_cols, width).transpose(0, 2, 1, 3)
    row_tiles = row_index + jnp.arange(tile_rows, dtype=jnp.int32) * rows_count
    col_tiles = column_position + jnp.arange(tile_cols, dtype=jnp.int32) * cols_count
    slots = (PANELS - 1) // cols_count + 1
    top_slots = (PANELS - 1) // rows_count + 1
    lost_column = lax.all_gather(failed, "col", axis=0, tiled=True)[0]
    lost = column_position == lost_column
    gathered = lax.all_gather(own[:, :slots], "col", axis=0)
    ids = jnp.arange(cols_count, dtype=jnp.int32).reshape(-1, 1, 1, 1, 1)
    others = jnp.sum(jnp.where(ids != lost_column, gathered, 0.0), axis=0)
    patch = totals[:, :slots] - others
    panels = []
    for k in range(PANELS):
        slot = k // cols_count
        panels.append(
            jnp.where(
                lost_column == k % cols_count, patch[:, slot], gathered[k % cols_count, :, slot]
            )
        )
    lead = jnp.stack(
        [
            jnp.where(
                row_index == i % rows_count,
                jnp.stack(
                    [panels[k][i // rows_count] for k in range(i + 1)]
                    + [jnp.zeros((width, width), jnp.float32) for _ in range(i + 1, PANELS)]
                ),
                0.0,
            )
            for i in range(PANELS)
        ]
    )
    lead = lax.psum(lead, "row")
    need = [
        tile_cols if a < top_slots else min(tile_cols, (rows_count * (a + 1) - 1) // cols_count + 1)
        for a in range(tile_rows)
    ]
    packed = jnp.concatenate([own[a, : need[a]] for a in range(tile_rows)], axis=0)
    lead_done, packed = lax.optimization_barrier((lead, packed))
    lead = lead_done
    summed = lax.psum(jnp.where(lost, 0.0, packed), "col")
    filled = []
    start = 0
    for a in range(tile_rows):
        pad = jnp.zeros((tile_cols - need[a], width, width), jnp.float32)
        filled.append(jnp.concatenate([summed[start : start + need[a]], pad], axis=0))
        start += need[a]
    work = jnp.where(lost, totals - jnp.stack(filled), own)
    tops = jnp.stack(
        [
            jnp.where(
                row_index == i % rows_count,
                jnp.concatenate([work[i // rows_count], totals[i // rows_count]], axis=0),
                0.0,
            )
            for i in range(PANELS)
        ]
    )
    tops = lax.psum(tops, "row")
    identity = jnp.eye(width, dtype=jnp.float32)
    factor = {}
    inverse = []
    for k in range(PANELS):
        for i in range(k, PANELS):
            tile = lead[i, k]
            for m in range(k):
                tile = tile - dot_t(factor[i, m], factor[k, m])
            if i == k:
                factor[k, k] = jnp.linalg.cholesky(tile)
                inverse.append(
                    jax.scipy.linalg.solve_triangular(factor[k, k], identity, lower=True)
                )
            else:
                factor[i, k] = dot_t(tile, inverse[k])
    solved_rows = []
    for k in range(PANELS):
        block = panels[k].reshape(tile_rows * width, width)
        for m in range(k):
            block = block - dot_t(solved_rows[m], factor[k, m])
        block = dot_t(block, inverse[k]).reshape(tile_rows, width, width)
        block = jnp.where((row_tiles > k)[:, None, None], block, 0.0)
        block = jnp.where((row_tiles == k)[:, None, None], factor[k, k][None], block)
        solved_rows.append(block.reshape(tile_rows * width, width))
    flat = tops.transpose(0, 2, 1, 3).reshape(PANELS, width, 2 * tile_cols * width)
    solved_cols = []
    for k in range(PANELS):
        block = flat[k]
        for m in range(k):
            block = block - dot(factor[k, m], solved_cols[m])
        solved_cols.append(dot(inverse[k], block))
    rows_factor = jnp.concatenate(solved_rows, axis=1)
    cols_factor = jnp.concatenate(solved_cols, axis=0)
    split = tile_cols * width
    shape = (tile_rows, width, tile_cols, width)
    update = dot(rows_factor, cols_factor[:, :split], FAST).reshape(shape).transpose(0, 2, 1, 3)
    drop = dot(rows_factor, cols_factor[:, split:], FAST).reshape(shape).transpose(0, 2, 1, 3)
    new_totals = (totals - drop).transpose(0, 2, 1, 3)
    work = work - update
    front = []
    for b in range(slots):
        tiles = work[:, b]
        for k in range(PANELS):
            if k // cols_count == b:
                mine = solved_rows[k].reshape(tile_rows, width, width)
                tiles = jnp.where(column_position == k % cols_count, mine, tiles)
        front.append(tiles)
    work = jnp.concatenate([jnp.stack(front, axis=1), work[:, slots:]], axis=1)
    keep = (row_tiles[:, None] >= col_tiles[None, :])[:, :, None, None]
    factored = jnp.where(keep, work, 0.0).transpose(0, 2, 1, 3)
    return (factored.reshape(matrix.shape), new_totals.reshape(checksum.shape))


def solution(mesh):
    return jax.shard_map(
        shards,
        mesh=mesh,
        in_specs=(
            P("row", None, None, "col", None, None),
            P("row", None, None, None, None),
            P("col"),
        ),
        out_specs=(P("row", None, None, "col", None, None), P("row", None, None, None, None)),
        check_vma=False,
    )
```

profile of v0, /device:TPU:0, one launch (start us, length us, event | category | flops | bytes accessed | tf_op | source)
XLA Modules:
  0.0 600.1 jit_solution(15367717784824096456)
XLA Ops:
  7.2 12.1 %copy.79 = f32[1,3,256,1,6,256]{2,5,4,1,3,0:T(8,128)} copy(f32[1,3,256,1,6,256]{5,3,4,2,1,0:T(1,128)} %param.6) | data formatting | bytes 9437184 | tf_op args[0]
  23.7 9.9 %all-reduce.2 = s32[4]{0:T(128)S(1)} all-reduce(s32[4]{0:T(128)S(1)} %dynamic-update-slice.10), channel_id=1, replica_groups=mesh['row'=8,'col'=4] {'col'}, use_global_device_ids=true, to_apply=%add.2 | all-reduce | flops 4 | bytes 32
  44.4 43.6 %all-gather.3.cloned.1.call-done = f32[12,1,256,256]{3,2,1,0:T(8,128)} async-done(((f32[3,1,256,256]{3,2,1,0:T(8,128)}), f32[12,1,256,256]{3,2,1,0:T(8,128)}) %all-gather.3.cloned.1.call-update) | async-done | bytes 3145744 | tf_op jit(solution)/shard_map/all_gather | solution.py:33
  114.0 52.6 %all-reduce.7.cloned.1.call-done = f32[3,3,256,256]{2,3,1,0:T(8,128)} async-done(((f32[3,3,256,256]{2,3,1,0:T(8,128)}), f32[3,3,256,256]{2,3,1,0:T(8,128)}) %all-reduce.7.cloned.1.call-update) | async-done | bytes 2359312 | tf_op jit(solution)/shard_map/psum | solution.py:58
  173.6 11.7 %cholesky.172 = f32[128,128]{1,0:T(8,128)S(1)} custom-call(f32[128,128]{1,0:T(8,128)S(1)} %cholesky.270), custom_call_target="Cholesky" | custom-call | tf_op jit(solution)/shard_map/jit(cholesky)/cholesky | solution.py:94
  185.4 9.8 %custom-call.15 = f32[1,128,128]{1,2,0:T(8,128)S(1)} custom-call(f32[1,128,128]{2,1,0:T(8,128)S(1)} %get-tuple-element.105), custom_call_target="InvertDiagBlocksLowerTriangular" | custom-call | tf_op jit(solution)/shard_map/jit(cholesky)/cholesky | solution.py:94
  195.7 11.7 %cholesky.189 = f32[128,128]{1,0:T(8,128)S(1)} custom-call(f32[128,128]{1,0:T(8,128)S(1)} %convolution_subtract_fusion.15), custom_call_target="Cholesky" | custom-call | tf_op jit(solution)/shard_map/jit(cholesky)/cholesky | solution.py:94
  214.0 20.1 %custom-call.16 = f32[2,128,128]{1,2,0:T(8,128)S(1)} custom-call(f32[2,128,128]{2,1,0:T(8,128)S(1)} %get-tuple-element.28), custom_call_target="InvertDiagBlocksLowerTriangular" | custom-call | tf_op jit(solution)/shard_map/jit(_solve_triangular)/triangular_solve | solution.py:96
  238.1 11.7 %cholesky.206 = f32[128,128]{1,0:T(8,128)S(1)} custom-call(f32[128,128]{1,0:T(8,128)S(1)} %cholesky.273), custom_call_target="Cholesky" | custom-call | tf_op jit(solution)/shard_map/jit(cholesky)/cholesky | solution.py:94
  249.9 9.8 %custom-call.17 = f32[1,128,128]{1,2,0:T(8,128)S(1)} custom-call(f32[1,128,128]{2,1,0:T(8,128)S(1)} %get-tuple-element.101), custom_call_target="InvertDiagBlocksLowerTriangular" | custom-call | tf_op jit(solution)/shard_map/jit(cholesky)/cholesky | solution.py:94
  260.2 11.7 %cholesky.223 = f32[128,128]{1,0:T(8,128)S(1)} custom-call(f32[128,128]{1,0:T(8,128)S(1)} %convolution_subtract_fusion.14), custom_call_target="Cholesky" | custom-call | tf_op jit(solution)/shard_map/jit(cholesky)/cholesky | solution.py:94
  279.6 19.9 %custom-call.18 = f32[2,128,128]{1,2,0:T(8,128)S(1)} custom-call(f32[2,128,128]{2,1,0:T(8,128)S(1)} %get-tuple-element.29), custom_call_target="InvertDiagBlocksLowerTriangular" | custom-call | tf_op jit(solution)/shard_map/jit(_solve_triangular)/triangular_solve | solution.py:96
  304.8 20.6 %all-reduce.9.cloned.1.call-done = f32[16,256,256]{1,2,0:T(8,128)} async-done(((f32[16,256,256]{1,2,0:T(8,128)}), f32[16,256,256]{1,2,0:T(8,128)}) %all-reduce.9.cloned.1.call-update) | async-done | bytes 4194320 | tf_op jit(solution)/shard_map/psum | solution.py:66
  345.1 11.7 %cholesky.240 = f32[128,128]{1,0:T(8,128)S(1)} custom-call(f32[128,128]{1,0:T(8,128)S(1)} %cholesky.276), custom_call_target="Cholesky" | custom-call | tf_op jit(solution)/shard_map/jit(cholesky)/cholesky | solution.py:94
  356.9 10.2 %custom-call.19 = f32[1,128,128]{1,2,0:T(8,128)S(1)} custom-call(f32[1,128,128]{2,1,0:T(8,128)S(1)} %get-tuple-element.97), custom_call_target="InvertDiagBlocksLowerTriangular" | custom-call | tf_op jit(solution)/shard_map/jit(cholesky)/cholesky | solution.py:94
  367.5 11.7 %cholesky.257 = f32[128,128]{1,0:T(8,128)S(1)} custom-call(f32[128,128]{1,0:T(8,128)S(1)} %convolution_subtract_fusion.13), custom_call_target="Cholesky" | custom-call | tf_op jit(solution)/shard_map/jit(cholesky)/cholesky | solution.py:94
  386.6 20.3 %custom-call.20 = f32[2,128,128]{1,2,0:T(8,128)} custom-call(f32[2,128,128]{2,1,0:T(8,128)S(1)} %get-tuple-element.30), custom_call_target="InvertDiagBlocksLowerTriangular" | custom-call | tf_op jit(solution)/shard_map/jit(_solve_triangular)/triangular_solve | solution.py:96
  427.0 51.3 %all-reduce.11.cloned.1.call-done = f32[3,256,12,256]{1,3,2,0:T(8,128)} async-done(((f32[3,256,12,256]{1,3,2,0:T(8,128)}), f32[3,256,12,256]{1,3,2,0:T(8,128)}) %all-reduce.11.cloned.1.call-update) | async-done | bytes 9437200 | tf_op jit(solution)/shard_map/psum | solution.py:84
  478.3 7.5 %fusion.83 = (f32[1,256,12,256]{1,3,2,0:T(8,128)}, f32[1,256,12,256]{1,3,2,0:T(8,128)S(1)}, f32[1,256,12,256]{1,3,2,0:T(8,128)}) fusion(f32[3,256,12,256]{1,3,2,0:T(8,128)} %all-reduce.11.cloned.1.call-done), kind=kLoop, calls=%fused_computation.179 | loop fusion | bytes 18874368 | tf_op jit(solution)/shard_map/slice | solution.py:112
  515.6 7.7 %pad_maximum_fusion = f32[768,3072]{1,0:T(8,128)} fusion(f32[256,3072]{1,0:T(8,128)} %fusion.32, f32[256,3072]{1,0:T(8,128)} %copy-done, f32[256,3072]{1,0:T(8,128)S(1)} %fusion.37), kind=kLoop, calls=%fused_computation.7 | loop fusion | flops 4718592 | bytes 18874368 | tf_op jit(solution)/shard_map/concatenate | solution.py:117
  523.3 10.0 %fusion.2 = f32[768,1536]{1,0:T(8,128)} fusion(f32[768,3072]{1,0:T(8,128)} %pad_maximum_fusion, f32[768,256]{1,0:T(8,128)} %get-tuple-element.114, f32[768,256]{1,0:T(8,128)} %get-tuple-element.112, f32[768,256]{1,0:T(8,128)} %bitcast.226), kind=kOutput, calls=%fused_computation.11 | convolution fusion | flops 5436997632 | bytes 11796480 | tf_op jit(solution)/shard_map/dot_general | solution.py:16
  533.3 7.7 %fusion = f32[768,1536]{1,0:T(8,128)} fusion(f32[768,3072]{1,0:T(8,128)S(1)} %copy-done.5, f32[768,256]{1,0:T(8,128)S(1)} %copy-done.39, f32[768,256]{1,0:T(8,128)S(1)} %copy-done.24, f32[768,256]{1,0:T(8,128)S(1)} %bitcast.227), kind=kOutput, calls=%fused_computation.9 | convolution fusion | flops 5436997632 | bytes 11796480 | tf_op jit(solution)/shard_map/dot_general | solution.py:16
  563.3 12.1 %copy.109 = f32[1,3,256,1,6,256]{5,3,4,2,1,0:T(1,128)} copy(f32[1,3,256,1,6,256]{2,5,4,1,3,0:T(8,128)} %fusion.5) | data formatting | bytes 9437184
  582.5 7.2 %copy_subtract_fusion = f32[1,3,256,6,256]{4,3,2,1,0:T(8,128)S(1)} fusion(f32[1,3,256,6,256]{4,3,2,1,0:T(8,128)} %reshape.319, f32[1,3,256,6,256]{4,2,3,1,0:T(8,128)} %param.7), kind=kLoop, calls=%fused_computation.8 | loop fusion | flops 1179648 | bytes 14155776 | tf_op jit(solution)/shard_map/sub | solution.py:122
  (275 shorter events, 189.7 us)
Async XLA Ops:
  7.2 80.9 %all-gather.3.cloned.1.call-start = ((), (), s32[]{:S(2)}) async-start(), calls=%async_computation.3 | async-start | bytes 3932160 | tf_op jit(solution)/shard_map/all_gather | solution.py:33
  21.7 145.0 %all-reduce.7.cloned.1.call-start = ((), (), s32[]{:S(2)}) async-start(), calls=%async_computation | async-start | bytes 4718592 | tf_op jit(solution)/shard_map/psum | solution.py:58
  104.9 220.5 %all-reduce.9.cloned.1.call-start = ((), (), s32[]{:S(2)}) async-start(), calls=%async_computation.1 | async-start | bytes 8388608 | tf_op jit(solution)/shard_map/psum | solution.py:66
  105.0 194.8 %copy-start.13 = (f32[256,256]{1,0:T(8,128)}, f32[256,256]{1,0:T(8,128)S(1)}, u32[]{:S(2)}) copy-start(f32[256,256]{1,0:T(8,128)S(1)} %fusion.31) | copy-start | bytes 786436
  171.3 307.1 %all-reduce.11.cloned.1.call-start = ((), (), s32[]{:S(2)}) async-start(), calls=%async_computation.2 | async-start | bytes 18874368 | tf_op jit(solution)/shard_map/psum | solution.py:84
  235.0 172.1 %copy-start.18 = (f32[128,256]{1,0:T(8,128)}, f32[128,256]{1,0:T(8,128)S(1)}, u32[]{:S(2)}) copy-start(f32[128,256]{1,0:T(8,128)S(1)} %fusion.53) | copy-start | bytes 393220
  279.6 45.7 %copy-start.52 = (s32[2,2]{1,0:T(2,128)}, s32[2,2]{1,0:T(2,128)S(1)}, u32[]{:S(2)}) copy-start(s32[2,2]{1,0:T(2,128)S(1)} %get-tuple-element.277) | copy-start | bytes 52
  299.8 41.5 %copy-start.15 = (f32[128,256]{1,0:T(8,128)}, f32[128,256]{1,0:T(8,128)S(1)}, u32[]{:S(2)}) copy-start(f32[128,256]{1,0:T(8,128)S(1)} %fusion.40) | copy-start | bytes 393220
  302.6 119.8 %copy-start.4 = (f32[256,256]{1,0:T(8,128)}, f32[256,256]{1,0:T(8,128)S(1)}, u32[]{:S(2)}) copy-start(f32[256,256]{1,0:T(8,128)S(1)} %fusion.22) | copy-start | bytes 786436
  342.4 40.3 %copy-start.53 = (s32[2,2]{1,0:T(2,128)S(1)}, s32[2,2]{1,0:T(2,128)}, u32[]{:S(2)}) copy-start(s32[2,2]{1,0:T(2,128)} %copy-done.52) | copy-start | bytes 52
  343.0 80.3 %copy-start.10 = (f32[256,256]{1,0:T(8,128)}, f32[256,256]{1,0:T(8,128)S(1)}, u32[]{:S(2)}) copy-start(f32[256,256]{1,0:T(8,128)S(1)} %fusion.36) | copy-start | bytes 786436
  343.0 64.0 %copy-start.38 = (f32[256,256]{1,0:T(8,128)S(1)}, f32[256,256]{1,0:T(8,128)}, u32[]{:S(2)}) copy-start(f32[256,256]{1,0:T(8,128)} %get-tuple-element.68) | copy-start | bytes 786436
  344.5 62.6 %copy-start.50 = (pred[3]{0:T(512)(128)(4,1)S(1)}, pred[3]{0:T(512)(128)(4,1)}, u32[]{:S(2)}) copy-start(pred[3]{0:T(512)(128)(4,1)} %get-tuple-element.116) | copy-start | bytes 13
  344.5 62.6 %copy-start.51 = (pred[3]{0:T(512)(128)(4,1)S(1)}, pred[3]{0:T(512)(128)(4,1)}, u32[]{:S(2)}) copy-start(pred[3]{0:T(512)(128)(4,1)} %get-tuple-element.117) | copy-start | bytes 13
  386.6 20.4 %copy-start.32 = (f32[256,256]{1,0:T(8,128)}, f32[256,256]{1,0:T(8,128)S(1)}, u32[]{:S(2)}) copy-start(f32[256,256]{1,0:T(8,128)S(1)} %get-tuple-element.272) | copy-start | bytes 786436
  408.0 6.6 %copy-start.6 = (f32[3,256,256]{1,2,0:T(8,128)}, f32[3,256,256]{1,2,0:T(8,128)S(1)}, u32[]{:S(2)}) copy-start(f32[3,256,256]{1,2,0:T(8,128)S(1)} %fusion.9) | copy-start | bytes 2359300
  408.3 14.1 %copy-start.8 = (f32[3,256,256]{2,1,0:T(8,128)}, f32[3,256,256]{2,1,0:T(8,128)S(1)}, u32[]{:S(2)}) copy-start(f32[3,256,256]{2,1,0:T(8,128)S(1)} %copy.97) | copy-start | bytes 2359300
  412.6 6.3 %copy-start.14 = (f32[256,256]{1,0:T(8,128)S(1)}, f32[256,256]{1,0:T(8,128)}, u32[]{:S(2)}) copy-start(f32[256,256]{1,0:T(8,128)} %copy-done.13) | copy-start | bytes 786436
  414.6 7.8 %copy-start.22 = (f32[3,1,256,256]{3,2,0,1:T(8,128)S(1)}, f32[3,1,256,256]{3,2,0,1:T(8,128)}, u32[]{:S(2)}) copy-start(f32[3,1,256,256]{3,2,0,1:T(8,128)} %copy.93) | copy-start | bytes 2359300
  414.6 8.7 %copy-start.23 = (f32[768,256]{1,0:T(8,128)S(1)}, f32[768,256]{1,0:T(8,128)}, u32[]{:S(2)}) copy-start(f32[768,256]{1,0:T(8,128)} %get-tuple-element.112) | copy-start | bytes 2359300
  523.3 10.0 %copy-start.5 = (f32[768,3072]{1,0:T(8,128)S(1)}, f32[768,3072]{1,0:T(8,128)}, u32[]{:S(2)}) copy-start(f32[768,3072]{1,0:T(8,128)} %pad_maximum_fusion) | copy-start | bytes 28311556
  523.3 10.0 %copy-start.9 = (f32[3,256,256]{2,1,0:T(8,128)S(1)}, f32[3,256,256]{2,1,0:T(8,128)}, u32[]{:S(2)}) copy-start(f32[3,256,256]{2,1,0:T(8,128)} %copy-done.8) | copy-start | bytes 2359300
  523.3 10.0 %copy-start.24 = (f32[768,256]{1,0:T(8,128)S(1)}, f32[768,256]{1,0:T(8,128)}, u32[]{:S(2)}) copy-start(f32[768,256]{1,0:T(8,128)} %get-tuple-element.112) | copy-start | bytes 2359300
  523.3 10.0 %copy-start.39 = (f32[768,256]{1,0:T(8,128)S(1)}, f32[768,256]{1,0:T(8,128)}, u32[]{:S(2)}) copy-start(f32[768,256]{1,0:T(8,128)} %get-tuple-element.114) | copy-start | bytes 2359300
  (37 other events, 100.9 us)
Sparse Core Ops, SparseCore 0:
  21.8 66.1 all-gather.2
  105.0 61.5 all-reduce.6
  171.4 153.9 all-reduce.8
  341.5 136.7 all-reduce.10
where the time goes:
time: 606 us; the launch traced here: 600 us
  other arithmetic  213 us (35%)
  waiting for transfers between devices  168 us (28%)
  local copies, waits for them, and re-layouts  122 us (20%)
  matrix products  65.9 us (11%)
  between operations  19.8 us (3%)
  blocking collectives  9.92 us (2%)
    another operation x20, other arithmetic, shards(): factor[k, k] = jnp.linalg.cholesky(tile)  104 us
    another operation x7, other arithmetic, shards(): jax.scipy.linalg.solve_triangular(factor[k, k], identity, lower=True)  62.5 us
    psum x1, waiting for transfers between devices, shards(): lead = lax.psum(lead, 'row')  52.6 us
    psum x1, waiting for transfers between devices, shards(): tops = lax.psum(tops, 'row')  51.3 us
    unnamed x124, local copies, waits for them, and re-layouts  46.6 us
    all_gather x1, waiting for transfers between devices, shards(): gathered = lax.all_gather(own[:, :slots], 'col', axis=0)  43.6 us
    dot_general x8, matrix products, dot(): return lax.dot_general(a, b, (((1,), (0,)), ((), ())), precision=precision)  41.3 us
    psum x1, waiting for transfers between devices, shards(): summed = lax.psum(jnp.where(lost, 0.0, packed), 'col')  20.6 us
  transfers between devices with their start and end apart: 4, of which 4 were waited for; matrix products, arithmetic and copies ran while one was open for 39% of the time, Pallas kernels for 0%

commit v1 on v0

--- a/solution.py
+++ b/solution.py
@@ -6,6 +6,11 @@
 PANELS = 3
 EXACT = lax.Precision.HIGHEST
 FAST = lax.Precision.HIGH
+
+
+def step_on_members_all(arr_in):
+    v_now = lax.all_gather(arr_in, "row").sum(axis=0)
+    return v_now
 
 
 def dot_t(a, b, precision=EXACT):
@@ -55,7 +60,7 @@
             for i in range(PANELS)
         ]
     )
-    lead = lax.psum(lead, "row")
+    lead = step_on_members_all(lead)
     need = [
         tile_cols if a < top_slots else min(tile_cols, (rows_count * (a + 1) - 1) // cols_count + 1)
         for a in range(tile_rows)

time: 606 us -> 636 us (1.050)
  waiting for transfers between devices: 168 us -> 197 us
  other arithmetic: 213 us -> 228 us
  local copies, waits for them, and re-layouts: 122 us -> 110 us
    all_gather x0 -> x1, waiting for transfers between devices: none -> 85.4 us  [step_on_members_all(): v_now = lax.all_gather(arr_in, 'row').sum(axis=0)]
    psum x1 -> x0, waiting for transfers between devices: 52.6 us -> none  [shards(): lead = lax.psum(lead, 'row')]
    unnamed x124 -> x133, local copies, waits for them, and re-layouts: 46.6 us -> 35.2 us
    psum x1, waiting for transfers between devices: 20.6 us -> 10.1 us  [shards(): summed = lax.psum(jnp.where(lost, 0.0, packed), 'col')]
    slice x1 -> x4, local copies, waits for them, and re-layouts: 7.46 us -> 16.9 us  [shards(): block = flat[k]]
    reduce_sum x0 -> x1, other arithmetic: none -> 7.94 us  [step_on_members_all(): v_now = lax.all_gather(arr_in, 'row').sum(axis=0)]
    select_n x6 -> x0, local copies, waits for them, and re-layouts: 6.88 us -> none  [the longest x3 4.25 us: shards(): factor[k, k] = jnp.linalg.cholesky(tile)]
    another operation x22, local copies, waits for them, and re-layouts: 12 us -> 18.4 us  [shards(): jax.scipy.linalg.solve_triangular(factor[k, k], identity, lower=True)]
  transfers between devices with their start and end apart: 4 -> 4, of which waited for: 4 -> 4; matrix products, arithmetic and copies ran while one was open for 39% -> 38% of each run, Pallas kernels for 0% -> 0%
where the time goes in v1:
time: 636 us; the launch traced here: 629 us
  other arithmetic  228 us (36%)
  waiting for transfers between devices  197 us (31%)
  local copies, waits for them, and re-layouts  110 us (17%)
  matrix products  63.3 us (10%)
  between operations  19.7 us (3%)
  blocking collectives  9.92 us (2%)
    another operation x20, other arithmetic, shards(): factor[k, k] = jnp.linalg.cholesky(tile)  105 us
    all_gather x1, waiting for transfers between devices, step_on_members_all(): v_now = lax.all_gather(arr_in, 'row').sum(axis=0)  85.4 us
    another operation x7, other arithmetic, shards(): jax.scipy.linalg.solve_triangular(factor[k, k], identity, lower=True)  66.2 us
    psum x1, waiting for transfers between devices, shards(): tops = lax.psum(tops, 'row')  52.5 us
    all_gather x1, waiting for transfers between devices, shards(): gathered = lax.all_gather(own[:, :slots], 'col', axis=0)  49.1 us
    dot_general x8, matrix products, dot(): return lax.dot_general(a, b, (((1,), (0,)), ((), ())), precision=precision)  39.7 us
    unnamed x133, local copies, waits for them, and re-layouts  35.2 us
    another operation x22, local copies, waits for them, and re-layouts, shards(): jax.scipy.linalg.solve_triangular(factor[k, k], identity, lower=True)  18.4 us
  transfers between devices with their start and end apart: 4, of which 4 were waited for; matrix products, arithmetic and copies ran while one was open for 38% of the time, Pallas kernels for 0%

profile of v1, /device:TPU:0, one launch (start us, length us, event | category | flops | bytes accessed | tf_op | source)
XLA Modules:
  0.0 629.4 jit_solution(950692530796132830)
XLA Ops:
  15.4 9.9 %all-reduce.2 = s32[4]{0:T(128)S(1)} all-reduce(s32[4]{0:T(128)S(1)} %dynamic-update-slice.10), channel_id=1, replica_groups=mesh['row'=8,'col'=4] {'col'}, use_global_device_ids=true, to_apply=%add.2 | all-reduce | flops 4 | bytes 32
  30.5 49.1 %all-gather.5.cloned.1.call-done = f32[12,1,256,256]{3,2,1,0:T(8,128)} async-done(((f32[3,1,256,256]{3,2,1,0:T(8,128)}), f32[12,1,256,256]{3,2,1,0:T(8,128)}) %all-gather.5.cloned.1.call-update) | async-done | bytes 3145744 | tf_op jit(solution)/shard_map/all_gather | solution.py:38
  100.6 85.4 %all-gather.7.cloned.1.call-done = f32[24,3,256,256]{3,2,1,0:T(8,128)} async-done(((f32[3,3,256,256]{3,2,1,0:T(8,128)}), f32[24,3,256,256]{3,2,1,0:T(8,128)}) %all-gather.7.cloned.1.call-update) | async-done | bytes 18874384 | tf_op jit(solution)/shard_map/all_gather | solution.py:12
  186.0 7.9 %reduce_sum.22 = f32[3,3,256,256]{3,2,1,0:T(8,128)S(1)} reduce(f32[8,3,3,256,256]{4,3,2,1,0:T(8,128)} %bitcast.233, f32[]{:T(128)} %constant.84.clone.1), dimensions={0}, to_apply=%region_1.2 | reduce | flops 4128768 | bytes 21233668 | tf_op jit(solution)/shard_map/reduce_sum | solution.py:12
  202.9 11.7 %cholesky.172 = f32[128,128]{1,0:T(8,128)S(1)} custom-call(f32[128,128]{1,0:T(8,128)S(1)} %cholesky.270), custom_call_target="Cholesky" | custom-call | tf_op jit(solution)/shard_map/jit(cholesky)/cholesky | solution.py:99
  214.7 9.8 %custom-call.15 = f32[1,128,128]{1,2,0:T(8,128)S(1)} custom-call(f32[1,128,128]{2,1,0:T(8,128)S(1)} %get-tuple-element.100), custom_call_target="InvertDiagBlocksLowerTriangular" | custom-call | tf_op jit(solution)/shard_map/jit(cholesky)/cholesky | solution.py:99
  225.0 11.7 %cholesky.189 = f32[128,128]{1,0:T(8,128)S(1)} custom-call(f32[128,128]{1,0:T(8,128)S(1)} %convolution_subtract_fusion.15), custom_call_target="Cholesky" | custom-call | tf_op jit(solution)/shard_map/jit(cholesky)/cholesky | solution.py:99
  244.2 20.2 %custom-call.16 = f32[2,128,128]{1,2,0:T(8,128)S(1)} custom-call(f32[2,128,128]{2,1,0:T(8,128)S(1)} %get-tuple-element.28), custom_call_target="InvertDiagBlocksLowerTriangular" | custom-call | tf_op jit(solution)/shard_map/jit(_solve_triangular)/triangular_solve | solution.py:101
  269.7 11.7 %cholesky.206 = f32[128,128]{1,0:T(8,128)S(1)} custom-call(f32[128,128]{1,0:T(8,128)S(1)} %cholesky.273), custom_call_target="Cholesky" | custom-call | tf_op jit(solution)/shard_map/jit(cholesky)/cholesky | solution.py:99
  282.0 10.4 %custom-call.17 = f32[1,128,128]{1,2,0:T(8,128)} custom-call(f32[1,128,128]{2,1,0:T(8,128)S(1)} %get-tuple-element.96), custom_call_target="InvertDiagBlocksLowerTriangular" | custom-call | tf_op jit(solution)/shard_map/jit(cholesky)/cholesky | solution.py:99
  294.6 11.7 %cholesky.223 = f32[128,128]{1,0:T(8,128)S(1)} custom-call(f32[128,128]{1,0:T(8,128)S(1)} %convolution_subtract_fusion.14), custom_call_target="Cholesky" | custom-call | tf_op jit(solution)/shard_map/jit(cholesky)/cholesky | solution.py:99
  318.1 20.6 %custom-call.18 = f32[2,128,128]{1,2,0:T(8,128)S(1)} custom-call(f32[2,128,128]{2,1,0:T(8,128)} %copy-done.48), custom_call_target="InvertDiagBlocksLowerTriangular" | custom-call | tf_op jit(solution)/shard_map/jit(_solve_triangular)/triangular_solve | solution.py:101
  342.8 10.1 %all-reduce.6.cloned.1.call-done = f32[16,256,256]{2,1,0:T(8,128)} async-done(((f32[16,256,256]{2,1,0:T(8,128)}), f32[16,256,256]{2,1,0:T(8,128)}) %all-reduce.6.cloned.1.call-update) | async-done | bytes 4194320 | tf_op jit(solution)/shard_map/psum | solution.py:71
  373.6 11.7 %cholesky.240 = f32[128,128]{1,0:T(8,128)S(1)} custom-call(f32[128,128]{1,0:T(8,128)S(1)} %cholesky.276), custom_call_target="Cholesky" | custom-call | tf_op jit(solution)/shard_map/jit(cholesky)/cholesky | solution.py:99
  385.4 9.8 %custom-call.19 = f32[1,128,128]{1,2,0:T(8,128)S(1)} custom-call(f32[1,128,128]{2,1,0:T(8,128)S(1)} %get-tuple-element.92), custom_call_target="InvertDiagBlocksLowerTriangular" | custom-call | tf_op jit(solution)/shard_map/jit(cholesky)/cholesky | solution.py:99
  397.4 12.1 %cholesky.257 = f32[128,128]{1,0:T(8,128)S(1)} custom-call(f32[128,128]{1,0:T(8,128)S(1)} %convolution_subtract_fusion.13), custom_call_target="Cholesky" | custom-call | tf_op jit(solution)/shard_map/jit(cholesky)/cholesky | solution.py:99
  414.6 8.3 %while.8 = (s32[]{:T(128)}, f32[256,256]{1,0:T(8,128)}, s32[2,2]{1,0:T(2,128)}, f32[2,128,128]{2,1,0:T(8,128)}, s32[]{:T(128)}) while((s32[]{:T(128)}, f32[256,256]{1,0:T(8,128)}, s32[2,2]{1,0:T(2,128)}, f32[2,128,128]{2,1,0:T(8,128)}, s32[]{:T(128)}) %tuple.105), condition=%wide.while_cond.clone.1, body=%wide.while_body.clone.1.sunk | while | flops 2 | bytes 132205 | solution.py:101
  422.9 21.1 %custom-call.20 = f32[2,128,128]{1,2,0:T(8,128)} custom-call(f32[2,128,128]{2,1,0:T(8,128)} %get-tuple-element.30), custom_call_target="InvertDiagBlocksLowerTriangular" | custom-call | tf_op jit(solution)/shard_map/jit(_solve_triangular)/triangular_solve | solution.py:101
  454.0 52.5 %all-reduce.8.cloned.1.call-done = f32[3,256,12,256]{3,1,0,2:T(8,128)} async-done(((f32[3,256,12,256]{3,1,0,2:T(8,128)}), f32[3,256,12,256]{3,1,0,2:T(8,128)}) %all-reduce.8.cloned.1.call-update) | async-done | bytes 9437200 | tf_op jit(solution)/shard_map/psum | solution.py:89
  506.5 7.4 %fusion.83 = (f32[1,256,12,256]{3,1,0,2:T(8,128)}, f32[1,256,12,256]{3,1,0,2:T(8,128)}, f32[1,256,12,256]{3,1,0,2:T(8,128)S(1)}) fusion(f32[3,256,12,256]{3,1,0,2:T(8,128)} %all-reduce.8.cloned.1.call-done), kind=kLoop, calls=%fused_computation.183 | loop fusion | bytes 18874368 | tf_op jit(solution)/shard_map/slice | solution.py:117
  552.3 7.6 %pad_maximum_fusion = f32[768,3072]{1,0:T(8,128)} fusion(f32[256,3072]{1,0:T(8,128)} %fusion.32, f32[256,3072]{1,0:T(8,128)} %copy-done, f32[256,3072]{1,0:T(8,128)S(1)} %fusion.37), kind=kLoop, calls=%fused_computation.7 | loop fusion | flops 4718592 | bytes 18874368 | tf_op jit(solution)/shard_map/concatenate | solution.py:122
  559.9 10.1 %fusion = f32[768,1536]{1,0:T(8,128)} fusion(f32[768,3072]{1,0:T(8,128)} %pad_maximum_fusion, f32[768,256]{1,0:T(8,128)} %get-tuple-element.109, f32[768,256]{1,0:T(8,128)} %copy-done.27, f32[768,256]{1,0:T(8,128)} %bitcast.242), kind=kOutput, calls=%fused_computation.9 | convolution fusion | flops 5436997632 | bytes 11796480 | tf_op jit(solution)/shard_map/dot_general | solution.py:21
  570.1 8.0 %fusion.2 = f32[768,1536]{1,0:T(8,128)} fusion(f32[768,3072]{1,0:T(8,128)S(1)} %copy-done.10, f32[768,256]{1,0:T(8,128)S(1)} %copy-done.46, f32[768,256]{1,0:T(8,128)S(1)} %copy-done.28, f32[768,256]{1,0:T(8,128)S(1)} %bitcast.243), kind=kOutput, calls=%fused_computation.11 | convolution fusion | flops 5436997632 | bytes 11796480 | tf_op jit(solution)/shard_map/dot_general | solution.py:21
  595.5 9.4 %copy.73 = f32[1,3,256,1,6,256]{5,3,4,2,1,0:T(1,128)} copy(f32[1,3,256,1,6,256]{5,2,1,4,3,0:T(8,128)} %fusion.5) | data formatting | bytes 9437184
  (278 shorter events, 198.9 us)
Async XLA Ops:
  7.2 6.9 %copy-start.60 = (u32[32]{0:T(128)S(1)}, u32[32]{0:T(128)}, u32[]{:S(2)}) copy-start(u32[32]{0:T(128)} %constant.117) | copy-start | bytes 388
  7.2 72.5 %all-gather.5.cloned.1.call-start = ((), (), s32[]{:S(2)}) async-start(), calls=%async_computation.2 | async-start | bytes 3932160 | tf_op jit(solution)/shard_map/all_gather | solution.py:38
  13.4 172.6 %all-gather.7.cloned.1.call-start = ((), (), s32[]{:S(2)}) async-start(), calls=%async_computation.3 | async-start | bytes 21233664 | tf_op jit(solution)/shard_map/all_gather | solution.py:12
  88.6 264.3 %all-reduce.6.cloned.1.call-start = ((), (), s32[]{:S(2)}) async-start(), calls=%async_computation | async-start | bytes 8388608 | tf_op jit(solution)/shard_map/psum | solution.py:71
  91.5 6.0 copy-start.52
  92.2 5.2 copy-start.54
  92.2 5.2 copy-start.56
  198.5 307.9 %all-reduce.8.cloned.1.call-start = ((), (), s32[]{:S(2)}) async-start(), calls=%async_computation.1 | async-start | bytes 18874368 | tf_op jit(solution)/shard_map/psum | solution.py:89
  265.4 75.8 %copy-start.23 = (f32[128,256]{1,0:T(8,128)}, f32[128,256]{1,0:T(8,128)S(1)}, u32[]{:S(2)}) copy-start(f32[128,256]{1,0:T(8,128)S(1)} %fusion.53) | copy-start | bytes 393220
  341.6 108.6 %copy-start.8 = (f32[256,256]{1,0:T(8,128)}, f32[256,256]{1,0:T(8,128)S(1)}, u32[]{:S(2)}) copy-start(f32[256,256]{1,0:T(8,128)S(1)} %fusion.22) | copy-start | bytes 786436
  370.8 80.3 %copy-start.11 = (f32[256,256]{1,0:T(8,128)}, f32[256,256]{1,0:T(8,128)S(1)}, u32[]{:S(2)}) copy-start(f32[256,256]{1,0:T(8,128)S(1)} %fusion.36) | copy-start | bytes 786436
  370.8 73.2 %copy-start.19 = (f32[3,1,256,256]{3,2,0,1:T(8,128)S(1)}, f32[3,1,256,256]{3,2,0,1:T(8,128)}, u32[]{:S(2)}) copy-start(f32[3,1,256,256]{3,2,0,1:T(8,128)} %copy-done.18) | copy-start | bytes 2359300
  370.8 73.2 %copy-start.24 = (f32[128,256]{1,0:T(8,128)S(1)}, f32[128,256]{1,0:T(8,128)}, u32[]{:S(2)}) copy-start(f32[128,256]{1,0:T(8,128)} %copy-done.23) | copy-start | bytes 393220
  372.7 73.1 %copy-start.17 = (f32[3,1,256,256]{3,2,0,1:T(8,128)S(1)}, f32[3,1,256,256]{3,2,0,1:T(8,128)}, u32[]{:S(2)}) copy-start(f32[3,1,256,256]{3,2,0,1:T(8,128)} %copy-done.16) | copy-start | bytes 2359300
  412.1 34.6 %copy-start.29 = (f32[256,256]{1,0:T(8,128)S(1)}, f32[256,256]{1,0:T(8,128)}, u32[]{:S(2)}) copy-start(f32[256,256]{1,0:T(8,128)} %get-tuple-element.64) | copy-start | bytes 786436
  413.8 38.1 %copy-start.31 = (f32[256,256]{1,0:T(8,128)}, f32[256,256]{1,0:T(8,128)S(1)}, u32[]{:S(2)}) copy-start(f32[256,256]{1,0:T(8,128)S(1)} %get-tuple-element.62) | copy-start | bytes 786436
  445.8 4.4 copy-start.5
  445.8 4.4 copy-start.15
  530.5 4.9 copy-start.4
  530.5 4.9 copy-start.9
  559.9 10.1 %copy-start.6 = (f32[3,256,256]{2,1,0:T(8,128)S(1)}, f32[3,256,256]{2,1,0:T(8,128)}, u32[]{:S(2)}) copy-start(f32[3,256,256]{2,1,0:T(8,128)} %copy-done.5) | copy-start | bytes 2359300
  559.9 10.1 %copy-start.10 = (f32[768,3072]{1,0:T(8,128)S(1)}, f32[768,3072]{1,0:T(8,128)}, u32[]{:S(2)}) copy-start(f32[768,3072]{1,0:T(8,128)} %pad_maximum_fusion) | copy-start | bytes 28311556
  559.9 10.1 %copy-start.28 = (f32[768,256]{1,0:T(8,128)S(1)}, f32[768,256]{1,0:T(8,128)}, u32[]{:S(2)}) copy-start(f32[768,256]{1,0:T(8,128)} %copy-done.27) | copy-start | bytes 2359300
  559.9 10.1 %copy-start.46 = (f32[768,256]{1,0:T(8,128)S(1)}, f32[768,256]{1,0:T(8,128)}, u32[]{:S(2)}) copy-start(f32[768,256]{1,0:T(8,128)} %get-tuple-element.109) | copy-start | bytes 2359300
  (43 other events, 84.8 us)
Sparse Core Ops, SparseCore 0:
  13.5 66.1 all-gather.4
  88.7 97.2 all-gather.6
  198.7 154.1 all-reduce.5
  369.4 136.9 all-reduce.7
